TPU v7x, 128 devices: a whole 4x4x4 slice. The times are simulated.
128 devices in a mesh: req: 16 (over x, z), ep: 8 (over y, core).
Axes of the slice: x: 4, y: 4, z: 4, core: 2. Of those that a mesh axis runs over, the one named last changes fastest.
Arguments:
- hidden: bfloat16 [16384, 1536], P(('req', 'ep')), may hold values from -6 to 6
- parents: int32 [256, 64], P(('req', 'ep')), may hold values from 0 to 62, as said below
- path: int32 [256, 64], P(('req', 'ep')), may hold values from -1 to 63, as said below
- cache_len: int32 [256], P(('req', 'ep')), may hold values from 64 to 1024
- page_table: int32 [256, 8], P(('req', 'ep')), may hold values from 0 to 15, as said below
- kv_pool: bfloat16 [2048, 128, 512], P(('req', 'ep')), may hold values from -90 to 90
- mig_slot: int32 [128], P(('req', 'ep')), may hold values from 0 to 1
- mig_dest: int32 [128], P(('req', 'ep')), may hold values from 0 to 7, as said below
- attn_gain: bfloat16 [1536], replicated, may hold values from 0.25 to 1.75
- w_qkv: bfloat16 [1536, 2048], replicated, may hold values from -0.15625 to 0.15625
- w_out: bfloat16 [1536, 1536], replicated, may hold values from -0.15625 to 0.15625
- moe_gain: bfloat16 [1536], replicated, may hold values from 0.25 to 1.75
- w_router: bfloat16 [1536, 32], replicated, may hold values from -0.15625 to 0.15625
- expert_ids: int32 [16384, 4], P(('req', 'ep')), may hold values from 0 to 31, all different within a row; in each aligned block of 128 rows (0 to 127, 128 to 255, ...) at most 32 rows name the same one
- w_gate: bfloat16 [128, 1536, 192], P(('req', 'ep')), may hold values from -0.15625 to 0.15625
- w_up: bfloat16 [128, 1536, 192], P(('req', 'ep')), may hold values from -0.15625 to 0.15625
- w_down: bfloat16 [128, 192, 1536], P(('req', 'ep')), may hold values from -0.21875 to 0.21875
Outputs:
- layer_out: bfloat16 [16384, 1536], P(('req', 'ep'))
- compact_kv: bfloat16 [256, 64, 512], P(('req', 'ep'))
Inputs may be any that keep to these rules, and one draw needn't show every extreme that they name: parents[r, 0] = 0 marks the root; for i >= 1, parents[r, i] < i. `path`: row r lists a chain of the tree of parents[r] from the root 0 down to some token, each entry the parent of the next, then -1. `page_table`: the 2 requests of one device name each of its 16 pool pages once. `mig_dest`: within each index of req, the entries of its 8 devices form a permutation. `expert_ids`: each row names 4 different experts; among the rows of one device no expert is named by more than 32 rows.
All inputs are finite; a program needn't handle non-finite values.
Results may differ from a plain program's by a relative error of at most 0.015.
Values may be sent and summed in bfloat16 or wider, within the bound.
A program may use at most 128 MiB of HBM per device.

v0:
```python
import jax
import jax.numpy as jnp
from jax import lax
from jax.sharding import PartitionSpec as P

QUERY_HEADS = 12
KEY_VALUE_HEADS = 2
HEAD_SIZE = 128
CAP = 32


EPSILON = 1e-06
ROPE_BASE = 1000000.0
PRECISE = lax.Precision.HIGHEST
MASKED = -1e30


def rms_scale(values, scaling):
    widened = values.astype(jnp.float32)
    spread = jnp.mean(widened * widened, axis=-1, keepdims=True)
    return (widened * lax.rsqrt(spread + EPSILON) * scaling.astype(jnp.float32)).astype(
        jnp.bfloat16
    )


def ancestry(parent_row):
    length = parent_row.shape[-1]
    indices = jnp.arange(length, dtype=jnp.int32)
    linked = (parent_row[:, None] == indices[None, :]).astype(jnp.float32)
    reached = jnp.minimum(linked + jnp.eye(length, dtype=jnp.float32), 1.0)
    for repeat_index in range(max(1, (length - 1).bit_length())):
        reached = jnp.minimum(jnp.dot(reached, reached, precision=PRECISE), 1.0)
    return reached


def apply_rotary(tensor, token_positions):
    halfway = tensor.shape[-1] // 2
    spectrum = ROPE_BASE ** (-2.0 * jnp.arange(halfway, dtype=jnp.float32) / tensor.shape[-1])
    angles = token_positions[..., None] * spectrum
    cosine = jnp.cos(angles)[..., None, :]
    sine_part = jnp.sin(angles)[..., None, :]
    former = tensor[..., :halfway]
    latter = tensor[..., halfway:]
    return jnp.concatenate(
        [former * cosine - latter * sine_part, latter * cosine + former * sine_part], axis=-1
    )


def take_rows(source_rows, row_ids):
    return source_rows[row_ids]


def split_into_heads(cache_rows, kv_heads):
    key_width = cache_rows.shape[-1] // 2
    leading = cache_rows.shape[:-1]
    head_shape = leading + (kv_heads, key_width // kv_heads)
    return (
        cache_rows[..., :key_width].reshape(head_shape),
        cache_rows[..., key_width:].reshape(head_shape),
    )


def attend(grouped_query, key_head_rows, value_head_rows, allowed):
    scores = jnp.einsum(
        "skgd,lkd->kgsl", grouped_query, key_head_rows, preferred_element_type=jnp.float32
    ) * grouped_query.shape[-1] ** (-0.5)
    scores = jnp.where(allowed[None, None], scores, MASKED)
    highest = jnp.max(scores, axis=-1)
    weights = jnp.exp(scores - highest[..., None])
    totals = jnp.sum(weights, axis=-1)
    summed = jnp.einsum(
        "kgsl,lkd->kgsd", weights, value_head_rows.astype(jnp.float32), precision=PRECISE
    )
    return (highest, totals, summed)


def blend(first_part, second_part):
    highest = jnp.maximum(first_part[0], second_part[0])
    first_factor = jnp.exp(first_part[0] - highest)
    second_factor = jnp.exp(second_part[0] - highest)
    totals = first_part[1] * first_factor + second_part[1] * second_factor
    summed = first_part[2] * first_factor[..., None] + second_part[2] * second_factor[..., None]
    return summed / totals[..., None]


def per_device(
    hidden,
    parents,
    path,
    cache_len,
    page_table,
    kv_pool,
    mig_slot,
    mig_dest,
    attn_gain,
    w_qkv,
    w_out,
    moe_gain,
    w_router,
    expert_ids,
    w_gate,
    w_up,
    w_down,
):
    cache_slot_count, draft_length = parents.shape
    req_count = lax.axis_size("req")
    ep_count = lax.axis_size("ep")
    device_count = req_count * ep_count
    query_width = w_out.shape[0]
    kv_width = kv_pool.shape[2]
    key_width = kv_width // 2
    context = page_table.shape[1] * kv_pool.shape[1]
    query_group_width = QUERY_HEADS // KEY_VALUE_HEADS
    model_dim = hidden.shape[1]
    tree_reach = jax.vmap(ancestry)(parents)
    tree_depth = jnp.sum(tree_reach, axis=-1) - 1.0
    leaving_slot = mig_slot[0]
    destination = mig_dest[0]
    ep_ids = jnp.arange(ep_count, dtype=jnp.int32)
    to_dest = ep_ids == destination
    own_cache = kv_pool[page_table].reshape(cache_slot_count, context, kv_width)
    leaving = lax.dynamic_index_in_dim(own_cache, leaving_slot, 0, keepdims=False)
    leave_len = lax.dynamic_index_in_dim(cache_len, leaving_slot, 0, keepdims=False)
    context_ids = jnp.arange(context, dtype=jnp.int32)
    normed = rms_scale(hidden, attn_gain)
    projected_input = jnp.dot(normed, w_qkv, preferred_element_type=jnp.float32).reshape(
        cache_slot_count, draft_length, -1
    )
    outgoing = jnp.where(to_dest[:, None, None], leaving[None], jnp.zeros((), jnp.bfloat16))
    length_out = jnp.where(to_dest, leave_len, 0)
    arrived_pages, arrived_lens = (
        lax.all_to_all(outgoing, "ep", split_axis=0, concat_axis=0, tiled=True),
        lax.all_to_all(length_out, "ep", split_axis=0, concat_axis=0, tiled=True),
    )
    anchor_ep = jnp.sum(jnp.where(arrived_lens > 0, ep_ids, 0))
    lengths = cache_len.at[leaving_slot].set(jnp.sum(arrived_lens))
    paged_caches = own_cache.at[leaving_slot].set(
        lax.dynamic_index_in_dim(arrived_pages, anchor_ep, 0, keepdims=False)
    )
    token_positions = lengths.astype(jnp.float32)[:, None] + tree_depth
    query_rows = apply_rotary(
        projected_input[..., :query_width].reshape(
            cache_slot_count, draft_length, QUERY_HEADS, HEAD_SIZE
        ),
        token_positions,
    ).astype(jnp.bfloat16)
    newest_keys = apply_rotary(
        projected_input[..., query_width : query_width + key_width].reshape(
            cache_slot_count, draft_length, KEY_VALUE_HEADS, HEAD_SIZE
        ),
        token_positions,
    ).astype(jnp.bfloat16)
    newest_values = projected_input[..., query_width + key_width :].astype(jnp.bfloat16)
    query_rows, newest_keys, newest_values = (
        query_rows.reshape(
            cache_slot_count, draft_length, KEY_VALUE_HEADS, query_group_width, HEAD_SIZE
        ),
        newest_keys,
        newest_values.reshape(cache_slot_count, draft_length, KEY_VALUE_HEADS, HEAD_SIZE),
    )
    stored_keys, stored_values = split_into_heads(paged_caches, KEY_VALUE_HEADS)
    cache_part = jax.vmap(attend)(
        query_rows,
        stored_keys,
        stored_values,
        jnp.broadcast_to(
            context_ids[None, None, :] < lengths[:, None, None],
            (cache_slot_count, draft_length, context),
        ),
    )
    draft_part = jax.vmap(attend)(query_rows, newest_keys, newest_values, tree_reach > 0.5)
    mixed = blend(cache_part, draft_part)
    attended = (
        jnp.transpose(mixed, (0, 3, 1, 2, 4))
        .reshape(cache_slot_count * draft_length, query_width)
        .astype(jnp.bfloat16)
    )
    projected_out = jnp.dot(attended, w_out, preferred_element_type=jnp.float32)
    residual_mid = (hidden.astype(jnp.float32) + projected_out).astype(jnp.bfloat16)
    fresh_kv = jnp.concatenate(
        [
            newest_keys.reshape(cache_slot_count, draft_length, key_width),
            newest_values.reshape(cache_slot_count, draft_length, key_width),
        ],
        axis=-1,
    )
    picked_kv = jax.vmap(take_rows)(fresh_kv, jnp.maximum(path, 0))
    compact_kv = jnp.where((path >= 0)[..., None], picked_kv, jnp.zeros((), jnp.bfloat16))
    normed_moe = rms_scale(residual_mid, moe_gain)
    logits = jnp.dot(normed_moe, w_router, preferred_element_type=jnp.float32)
    experts = w_router.shape[1]
    split = device_count // experts
    chosen = jnp.take_along_axis(logits, expert_ids, axis=1)
    squashed = jax.nn.sigmoid(chosen)
    gate_share = squashed / jnp.sum(squashed, axis=1, keepdims=True)
    marks = expert_ids[:, :, None] == jnp.arange(experts, dtype=jnp.int32)[None, None, :]
    assigned = jnp.sum(marks.astype(jnp.int32), axis=1)
    ranks = jnp.cumsum(assigned, axis=0) - assigned
    slot_ids = jnp.arange(CAP, dtype=jnp.int32)
    dispatch_table = (
        (ranks.T[:, None, :] == slot_ids[None, :, None]) & (assigned.T[:, None, :] > 0)
    ).astype(jnp.bfloat16)
    packed = jnp.einsum(
        "ect,td->ecd", dispatch_table, normed_moe, preferred_element_type=jnp.float32
    ).astype(jnp.bfloat16)
    outgoing_rows = jnp.repeat(packed, split, axis=0)
    tok_rows = lax.all_to_all(outgoing_rows, ("req", "ep"), split_axis=0, concat_axis=0, tiled=True)
    flat_rows = tok_rows.reshape(-1, model_dim)
    gate_val = jnp.dot(flat_rows, w_gate[0], preferred_element_type=jnp.float32)
    up_val = jnp.dot(flat_rows, w_up[0], preferred_element_type=jnp.float32)
    activated = (jnp.maximum(gate_val, 0.0) * up_val).astype(jnp.bfloat16)
    result = jnp.dot(activated, w_down[0], preferred_element_type=jnp.float32).astype(jnp.bfloat16)
    returned = lax.all_to_all(
        result.reshape(tok_rows.shape), ("req", "ep"), split_axis=0, concat_axis=0, tiled=True
    )
    expert_out = jnp.sum(
        returned.astype(jnp.float32).reshape(experts, split, CAP, model_dim), axis=1
    ).reshape(experts * CAP, model_dim)
    slot_pick = expert_ids * CAP + jnp.take_along_axis(ranks, expert_ids, axis=1)
    gathered_rows = expert_out[slot_pick]
    moe_sum = jnp.sum(gate_share[..., None] * gathered_rows, axis=1)
    layer_out = (residual_mid.astype(jnp.float32) + moe_sum).astype(jnp.bfloat16)
    return (layer_out, compact_kv)


def solution(mesh):
    in_specs = (
        P(("req", "ep"), None),
        P(("req", "ep"), None),
        P(("req", "ep"), None),
        P(("req", "ep")),
        P(("req", "ep"), None),
        P(("req", "ep"), None, None),
        P(("req", "ep")),
        P(("req", "ep")),
        P(),
        P(),
        P(),
        P(),
        P(),
        P(("req", "ep"), None),
        P(("req", "ep"), None, None),
        P(("req", "ep"), None, None),
        P(("req", "ep"), None, None),
    )
    out_specs = (P(("req", "ep"), None), P(("req", "ep"), None, None))
    return jax.shard_map(
        per_device, mesh=mesh, in_specs=in_specs, out_specs=out_specs, check_vma=False
    )
```

profile of v0, /device:TPU:9, one launch (start us, length us, event | category | flops | bytes accessed | tf_op | source)
XLA Modules:
  0.0 527.0 jit_solution(1400419293414899093)
XLA Ops:
  0.6 0.8 copy.199
  2.8 0.6 dynamic_slice.12
  3.4 1.2 compare_select_fusion
  4.6 5.2 all-to-all-start
  9.8 0.7 compare_select_fusion.3
  10.6 2.0 gather_fusion
  12.6 1.3 dynamic-slice_bitcast_fusion
  13.9 3.8 broadcast_select_fusion
  17.7 5.0 all-to-all-start.1
  23.0 3.8 fusion.33
  28.8 0.7 copy.167
  29.5 0.6 reshape.268
  30.4 0.8 and_reduce_fusion
  31.2 0.6 compare_bitcast_fusion
  32.2 0.6 select_reduce_fusion
  34.1 0.6 reduce_sum.103
  34.8 1.3 fusion.54
  36.2 0.3 multiply_cosine_fusion
  36.5 0.5 subtract_convert_fusion
  37.9 0.6 fusion.66
  38.8 76.7 %all-to-all-done.1 = bf16[8,1024,512]{2,1,0:T(8,128)(2,1)} async-done(((bf16[8,1024,512]{2,1,0:T(8,128)(2,1)}), bf16[8,1024,512]{2,1,0:T(8,128)(2,1)}, u32[]{:S(2)}, u32[]{:S(2)}) %all-to-all-start.1) | async-done | bytes 8388640 | tf_op jit(solution)/shard_map/all_to_all | solution.py:132
  115.5 3.5 select_dynamic-update-slice_fusion
  119.0 2.7 fusion.63
  121.7 1.7 copy.148
  123.3 1.3 copy.154
  124.7 1.3 bitcast_reduce_fusion
  125.9 1.6 fusion.2
  127.6 4.0 fusion.19
  131.6 1.1 fusion.22
  133.0 0.4 convert_element_type.79
  133.5 3.2 multiply_reduce_fusion.1
  136.7 2.7 convolution_convert_fusion.1
  139.4 8.0 %broadcast_in_dim.139 = bf16[32,4,32,1536]{3,2,1,0:T(8,128)(2,1)} broadcast(bf16[32,32,1536]{2,1,0:T(8,128)(2,1)} %convolution_convert_fusion.1), dimensions={0,2,3} | broadcast | bytes 15728640 | tf_op jit(solution)/shard_map/broadcast_in_dim | solution.py:206
  147.5 155.5 %all_to_all.21 = bf16[128,32,1536]{2,1,0:T(8,128)(2,1)S(1)} all-to-all(bf16[128,32,1536]{2,1,0:T(8,128)(2,1)} %bitcast.142), channel_id=1, replica_groups=mesh['req'=16,'ep'=8] {'req','ep'}, dimensions={0} | all-to-all | bytes 25165824 | tf_op jit(solution)/shard_map/all_to_all | solution.py:207
  302.9 4.5 copy-done.2
  307.4 6.0 %convolution_maximum_fusion = f32[4096,192]{0,1:T(8,128)} fusion(bf16[4096,1536]{1,0:T(8,128)(2,1)S(1)} %bitcast.140, bf16[1,1536,192]{1,2,0:T(8,128)(2,1)S(1)} %copy-done.23), kind=kOutput, calls=%fused_computation.14 | convolution fusion | flops 2416705536 | bytes 16318464 | tf_op jit(solution)/shard_map/dot_general | solution.py:209
  313.4 13.6 %convolution_convert_fusion = bf16[4096,1536]{1,0:T(8,128)(2,1)} fusion(f32[4096,192]{0,1:T(8,128)} %convolution_maximum_fusion, bf16[4096,1536]{1,0:T(8,128)(2,1)} %bitcast.141, bf16[1,192,1536]{2,1,0:T(8,128)(2,1)S(1)} %copy-done.12, bf16[1,1536,192]{1,2,0:T(8,128)(2,1)S(1)} %copy-done.6), kind=kOutput, calls=%fused_computation.6 | convolution fusion | flops 4839702528 | bytes 29491200 | tf_op jit(solution)/shard_map/dot_general | solution.py:212
  327.0 9.5 %all-to-all-start.3 = ((bf16[128,32,1536]{2,1,0:T(8,128)(2,1)}), bf16[128,32,1536]{2,1,0:T(8,128)(2,1)}, u32[]{:S(2)}, u32[]{:S(2)}) async-start(bf16[128,32,1536]{2,1,0:T(8,128)(2,1)} %bitcast.139), calls=%async_computation.3 | async-start | bytes 25165824 | tf_op jit(solution)/shard_map/all_to_all | solution.py:213
  336.9 3.8 gather_fusion.3
  341.3 1.3 gather_fusion.4
  342.6 0.7 broadcast_select_fusion.1
  343.6 3.8 gather_fusion.2
  347.8 151.6 %all-to-all-done.3 = bf16[128,32,1536]{2,1,0:T(8,128)(2,1)} async-done(((bf16[128,32,1536]{2,1,0:T(8,128)(2,1)}), bf16[128,32,1536]{2,1,0:T(8,128)(2,1)}, u32[]{:S(2)}, u32[]{:S(2)}) %all-to-all-start.3) | async-done | bytes 12582944 | tf_op jit(solution)/shard_map/all_to_all | solution.py:213
  499.4 10.2 %convert_reduce_fusion = f32[32,32,1536]{2,1,0:T(8,128)} fusion(bf16[128,32,1536]{2,1,0:T(8,128)(2,1)} %all-to-all-done.3), kind=kLoop, calls=%fused_computation.5 | loop fusion | flops 11010048 | bytes 18874368 | tf_op jit(solution)/shard_map/reduce_sum | solution.py:216
  509.6 7.6 %gather_fusion.1 = f32[512,1536]{1,0:T(8,128)} fusion(f32[1024,1536]{1,0:T(8,128)} %bitcast.138, s32[1024]{0:T(1024)S(1)} %pad_clamp_fusion), kind=kCustom, calls=%fused_computation.1 | custom fusion | bytes 6293504 | tf_op jit(solution)/shard_map/gather | solution.py:220
  517.1 4.8 reshape.287
  521.9 4.2 multiply_reduce_fusion
  526.1 0.9 add_convert_fusion.1
  (106 shorter events, 5.2 us)
Async XLA Ops:
  0.6 10.0 %copy-start = (bf16[16,128,512]{2,1,0:T(8,128)(2,1)S(1)}, bf16[16,128,512]{2,1,0:T(8,128)(2,1)}, u32[]{:S(2)}) copy-start(bf16[16,128,512]{2,1,0:T(8,128)(2,1)} %param.26) | copy-start | bytes 6291460
  4.6 13.2 %all-to-all-start = ((s32[8,1,1]{2,1,0:T(1,128)}), s32[8,1,1]{2,1,0:T(1,128)S(1)}, u32[]{:S(2)}, u32[]{:S(2)}) async-start(s32[8,1,1]{2,1,0:T(1,128)} %compare_select_fusion), calls=%async_computation | async-start | bytes 8192 | tf_op jit(solution)/shard_map/all_to_all | solution.py:133
  17.7 5.1 copy-start.18
  17.7 5.1 copy-start.3
  17.7 97.8 %all-to-all-start.1 = ((bf16[8,1024,512]{2,1,0:T(8,128)(2,1)}), bf16[8,1024,512]{2,1,0:T(8,128)(2,1)}, u32[]{:S(2)}, u32[]{:S(2)}) async-start(bf16[8,1024,512]{2,1,0:T(8,128)(2,1)} %broadcast_select_fusion), calls=%async_computation.1 | async-start | bytes 16777216 | tf_op jit(solution)/shard_map/all_to_all | solution.py:132
  22.8 4.2 copy-start.19
  22.8 4.2 copy-start.20
  22.8 5.7 %copy-start.16 = (s32[128,4]{0,1:T(4,128)S(1)}, s32[128,4]{0,1:T(4,128)}, u32[]{:S(2)}) copy-start(s32[128,4]{0,1:T(4,128)} %param.34) | copy-start | bytes 6148
  23.0 7.4 %copy-start.22 = (s32[3]{0:T(128)S(1)}, s32[3]{0:T(128)}, u32[]{:S(2)}) copy-start(s32[3]{0:T(128)} %constant.115.clone.1) | copy-start | bytes 40
  37.9 83.7 %copy-start.8 = (bf16[2,64,2,64]{3,1,2,0:T(8,128)(2,1)}, bf16[2,64,2,64]{3,1,2,0:T(8,128)(2,1)S(1)}, u32[]{:S(2)}) copy-start(bf16[2,64,2,64]{3,1,2,0:T(8,128)(2,1)S(1)} %get-tuple-element.33) | copy-start | bytes 98308
  37.9 83.7 %copy-start.10 = (bf16[2,64,2,64]{3,1,2,0:T(8,128)(2,1)}, bf16[2,64,2,64]{3,1,2,0:T(8,128)(2,1)S(1)}, u32[]{:S(2)}) copy-start(bf16[2,64,2,64]{3,1,2,0:T(8,128)(2,1)S(1)} %get-tuple-element.34) | copy-start | bytes 98308
  38.5 83.1 %copy-start.4 = (f32[2,2,6,64,64]{3,4,2,1,0:T(8,128)}, f32[2,2,6,64,64]{3,4,2,1,0:T(8,128)S(1)}, u32[]{:S(2)}) copy-start(f32[2,2,6,64,64]{3,4,2,1,0:T(8,128)S(1)} %get-tuple-element.44) | copy-start | bytes 1179652
  124.7 2.9 copy-start.7
  127.5 4.1 copy-start.5
  127.5 4.1 copy-start.15
  131.6 5.1 copy-start.14
  131.6 5.1 copy-start.17
  147.5 160.0 %copy-start.23 = (bf16[1,1536,192]{1,2,0:T(8,128)(2,1)S(1)}, bf16[1,1536,192]{1,2,0:T(8,128)(2,1)}, u32[]{:S(2)}) copy-start(bf16[1,1536,192]{1,2,0:T(8,128)(2,1)} %param.35) | copy-start | bytes 1769476
  302.9 4.5 copy-start.2
  307.4 6.0 %copy-start.6 = (bf16[1,1536,192]{1,2,0:T(8,128)(2,1)S(1)}, bf16[1,1536,192]{1,2,0:T(8,128)(2,1)}, u32[]{:S(2)}) copy-start(bf16[1,1536,192]{1,2,0:T(8,128)(2,1)} %param.36) | copy-start | bytes 1769476
  307.4 6.0 %copy-start.12 = (bf16[1,192,1536]{2,1,0:T(8,128)(2,1)S(1)}, bf16[1,192,1536]{2,1,0:T(8,128)(2,1)}, u32[]{:S(2)}) copy-start(bf16[1,192,1536]{2,1,0:T(8,128)(2,1)} %param.37) | copy-start | bytes 1769476
  327.0 9.5 %copy-start.21 = (s32[2,64]{1,0:T(2,128)S(1)}, s32[2,64]{1,0:T(2,128)}, u32[]{:S(2)}) copy-start(s32[2,64]{1,0:T(2,128)} %param.23) | copy-start | bytes 1540
  327.0 172.4 %all-to-all-start.3 = ((bf16[128,32,1536]{2,1,0:T(8,128)(2,1)}), bf16[128,32,1536]{2,1,0:T(8,128)(2,1)}, u32[]{:S(2)}, u32[]{:S(2)}) async-start(bf16[128,32,1536]{2,1,0:T(8,128)(2,1)} %bitcast.139), calls=%async_computation.3 | async-start | bytes 25165824 | tf_op jit(solution)/shard_map/all_to_all | solution.py:213
  336.9 4.3 copy-start.9
  336.9 4.3 copy-start.11
  336.9 6.5 %copy-start.13 = (bf16[1536,32]{0,1:T(8,128)(2,1)S(1)}, bf16[1536,32]{0,1:T(8,128)(2,1)}, u32[]{:S(2)}) copy-start(bf16[1536,32]{0,1:T(8,128)(2,1)} %param.33) | copy-start | bytes 294916
  509.6 17.4 %copy-start.1 = (bf16[16,128,512]{2,1,0:T(8,128)(2,1)S(1)}, bf16[16,128,512]{2,1,0:T(8,128)(2,1)}, u32[]{:S(2)}) copy-start(bf16[16,128,512]{2,1,0:T(8,128)(2,1)} %param.26) | copy-start | bytes 6291460
where the time goes:
time: 534 us; the launch traced here: 527 us
  waiting for transfers between devices  228 us (43%)
  blocking collectives  155 us (29%)
  local copies, waits for them, and re-layouts  48.2 us (9%)
  matrix products  37.9 us (7%)
  other arithmetic  32.7 us (6%)
  starting transfers between devices  19.8 us (4%)
    all_to_all x1, blocking collectives, per_device(): lax.all_to_all(outgoing_rows, ('req', 'ep'), split_axis=0, concat_axis=0,...  155 us
    all_to_all x1, waiting for transfers between devices, per_device(): lax.all_to_all(result.reshape(tok_rows.shape), ('req', 'ep'), split_axis=...  152 us
    all_to_all x1, waiting for transfers between devices, per_device(): lax.all_to_all(outgoing, 'ep', split_axis=0, concat_axis=0, tiled=True)  76.7 us
    dot_general x1, matrix products, per_device(): jnp.dot(activated, w_down[0], preferred_element_type=jnp.float32)  13.6 us
    gather x2, local copies, waits for them, and re-layouts, per_device(): gathered_rows = expert_out[slot_pick]  12.4 us
  transfers between devices with their start and end apart: 3, of which 2 were waited for; matrix products, arithmetic and copies ran while one was open for 6% of the time, Pallas kernels for 0%

commit v1 on v0

--- a/solution.py
+++ b/solution.py
@@ -1,6 +1,8 @@
 import jax
 import jax.numpy as jnp
 from jax import lax
+from jax.experimental import pallas as pl
+from jax.experimental.pallas import tpu as pltpu
 from jax.sharding import PartitionSpec as P
 
 QUERY_HEADS = 12
@@ -81,6 +83,280 @@
     totals = first_part[1] * first_factor + second_part[1] * second_factor
     summed = first_part[2] * first_factor[..., None] + second_part[2] * second_factor[..., None]
     return summed / totals[..., None]
+
+
+SLOTS = 1024
+ROUNDS = 64
+GROUPS = 4
+PER_GROUP = ROUNDS // GROUPS
+HALF_CAP = CAP // 2
+SHARD = 192
+MESH = pl.DeviceIdType.MESH
+
+
+def here():
+    req = lax.axis_index("req")
+    ep = lax.axis_index("ep")
+    return req // 4, req % 4, ep // 2, ep % 2
+
+
+def partner(place, turn, sign):
+    x, z, y, core = place
+    dx = (3 * turn) % 4
+    dz = (turn + turn // 4) % 4
+    other_pair = (turn + turn // 16) % 2
+    dcore = (turn // 2 + turn // 32) % 2
+    far_x = (x + sign * dx + 4) % 4
+    far_z = (z + sign * dz + 4) % 4
+    far_y = y * (1 - other_pair) + (3 - y) * other_pair
+    return far_x * 4 + far_z, far_y, (core + dcore) % 2
+
+
+def first_slot(req, y, core):
+    return pl.multiple_of((req * 2 + y // 2) * CAP + HALF_CAP * core, HALF_CAP)
+
+
+def for_each(low, high, act):
+    def body(index, carry):
+        act(index)
+        return carry
+
+    lax.fori_loop(low, high, body, 0)
+
+
+def experts_kernel(
+    normed_ref,
+    mid_ref,
+    ids_ref,
+    router_ref,
+    gate_up_ref,
+    down_ref,
+    out_ref,
+    packed,
+    arrived,
+    results,
+    returned,
+    gate_up,
+    down,
+    shares,
+    out_sem,
+    in_sem,
+    back_sem,
+    home_sem,
+    local_sem,
+    weight_send,
+    weight_recv,
+):
+    place = here()
+    x, z, y, core = place
+    req = lax.axis_index("req")
+    mate = (req, y * 2 + 1 - core)
+    pair_y = (y // 2) * 2 + 1 - y % 2
+    pair = (req, pair_y * 2 + core)
+
+    barrier = pltpu.get_barrier_semaphore()
+
+    def greet(turn):
+        far_req, far_y, far_core = partner(place, turn, 1)
+        pl.semaphore_signal(
+            barrier, inc=1, device_id=(far_req, far_y * 2 + far_core), device_id_type=MESH
+        )
+
+    for_each(1, ROUNDS, greet)
+    pl.semaphore_signal(barrier, inc=1, device_id=pair, device_id_type=MESH)
+
+    own_gate = pltpu.make_async_copy(gate_up_ref, gate_up.at[:, 0:384], local_sem.at[0])
+    own_low = pltpu.make_async_copy(
+        down_ref.at[pl.ds(0, 128)], down.at[pl.ds(0, 128)], local_sem.at[1]
+    )
+    own_high = pltpu.make_async_copy(
+        down_ref.at[pl.ds(128, 64)], down.at[pl.ds(256, 64)], local_sem.at[2]
+    )
+    own_gate.start()
+    own_low.start()
+    own_high.start()
+
+    tokens = ids_ref.shape[0]
+    experts = router_ref.shape[1]
+    normed = normed_ref[...]
+    logits = jnp.dot(normed, router_ref[...], preferred_element_type=jnp.float32)
+    lanes = lax.broadcasted_iota(jnp.int32, (tokens, experts), 1)
+    assigned = jnp.zeros((tokens, experts), jnp.float32)
+    for choice in range(ids_ref.shape[1]):
+        assigned += jnp.where(ids_ref[:, choice : choice + 1] == lanes, 1.0, 0.0)
+    earlier = lax.broadcasted_iota(jnp.int32, (tokens, tokens), 0) > lax.broadcasted_iota(
+        jnp.int32, (tokens, tokens), 1
+    )
+    ranks = jnp.dot(
+        jnp.where(earlier, 1.0, 0.0).astype(jnp.bfloat16),
+        assigned.astype(jnp.bfloat16),
+        preferred_element_type=jnp.float32,
+    )
+    slot_of = jnp.where(assigned > 0.5, ranks, -1.0).astype(jnp.bfloat16)
+    squashed = jnp.where(assigned > 0.5, 1.0 / (1.0 + jnp.exp(-logits)), 0.0)
+    share = squashed / jnp.sum(squashed, axis=1, keepdims=True)
+    share_high = share.astype(jnp.bfloat16)
+    share_low = (share - share_high.astype(jnp.float32)).astype(jnp.bfloat16)
+
+    quarter = SLOTS // GROUPS
+    slot_rows = lax.broadcasted_iota(jnp.int32, (quarter, experts), 0)
+    slot_lanes = lax.broadcasted_iota(jnp.int32, (quarter, experts), 1)
+    want = (lax.broadcasted_iota(jnp.int32, (quarter, tokens), 0) % CAP).astype(jnp.float32)
+    for part in range(GROUPS):
+        spread = jnp.where((slot_rows + part * quarter) // CAP == slot_lanes, 1.0, 0.0)
+        named = lax.dot_general(
+            spread.astype(jnp.bfloat16),
+            slot_of,
+            (((1,), (1,)), ((), ())),
+            preferred_element_type=jnp.float32,
+        )
+        table = jnp.where(named == want, 1.0, 0.0).astype(jnp.bfloat16)
+        packed[pl.ds(part * quarter, quarter), :] = jnp.dot(
+            table, normed, preferred_element_type=jnp.float32
+        ).astype(jnp.bfloat16)
+
+    pl.semaphore_wait(barrier, ROUNDS)
+
+    own_gate.wait()
+    own_low.wait()
+    own_high.wait()
+    GATE = [gate_up.at[:, pl.ds(384 * s, 384)] for s in range(4)]
+    LOW = [down.at[pl.ds(384 * (s // 2) + 128 * (s % 2), 128)] for s in range(4)]
+    HIGH = [down.at[pl.ds(384 * (s // 2) + 256 + 64 * (s % 2), 64)] for s in range(4)]
+
+    def weight_copies(source, target, device, base):
+        return [
+            pltpu.make_async_remote_copy(
+                src_ref=refs[source],
+                dst_ref=refs[target],
+                send_sem=weight_send.at[base + k],
+                recv_sem=weight_recv.at[base + k],
+                device_id=device,
+                device_id_type=MESH,
+            )
+            for k, refs in enumerate((GATE, LOW, HIGH))
+        ]
+
+    to_pair = weight_copies(0, 2, pair, 0)
+    to_mate = weight_copies(0, 1, mate, 3)
+    relay = weight_copies(2, 3, mate, 6)
+
+    def outward(turn):
+        far_req, far_y, far_core = partner(place, turn, 1)
+        return pltpu.make_async_remote_copy(
+            src_ref=packed.at[pl.ds(first_slot(far_req, far_y, far_core), HALF_CAP)],
+            dst_ref=arrived.at[pl.ds(pl.multiple_of(turn * HALF_CAP, HALF_CAP), HALF_CAP)],
+            send_sem=out_sem.at[turn],
+            recv_sem=in_sem.at[turn],
+            device_id=(far_req, far_y * 2 + far_core),
+            device_id_type=MESH,
+        )
+
+    def homeward(turn):
+        far_req, far_y, far_core = partner(place, turn, -1)
+        return pltpu.make_async_remote_copy(
+            src_ref=results.at[pl.ds(pl.multiple_of(turn * HALF_CAP, HALF_CAP), HALF_CAP)],
+            dst_ref=returned.at[pl.ds(first_slot(req, y, core), HALF_CAP)],
+            send_sem=back_sem.at[turn],
+            recv_sem=home_sem.at[turn],
+            device_id=(far_req, far_y * 2 + far_core),
+            device_id_type=MESH,
+        )
+
+    for copy in to_pair + to_mate:
+        copy.start()
+    for_each(1, ROUNDS, lambda turn: outward(turn).start())
+    mine = first_slot(req, y, core)
+    keep = pltpu.make_async_copy(
+        packed.at[pl.ds(mine, HALF_CAP)], arrived.at[pl.ds(0, HALF_CAP)], local_sem.at[0]
+    )
+    keep.start()
+
+    spread_rows = lax.broadcasted_iota(jnp.int32, (experts, SLOTS), 0)
+    spread_lanes = lax.broadcasted_iota(jnp.int32, (experts, SLOTS), 1)
+    spread = jnp.where(spread_lanes // CAP == spread_rows, 1.0, 0.0).astype(jnp.bfloat16)
+    slot_lane = (lax.broadcasted_iota(jnp.int32, (tokens, SLOTS), 1) % CAP).astype(jnp.float32)
+    chosen = jnp.dot(slot_of, spread, preferred_element_type=jnp.float32) == slot_lane
+    for half, part in enumerate((share_high, share_low)):
+        shares[pl.ds(half * tokens, tokens), :] = jnp.where(
+            chosen, jnp.dot(part, spread, preferred_element_type=jnp.float32), 0.0
+        ).astype(jnp.bfloat16)
+
+    keep.wait()
+    for sent, passed in zip(to_pair, relay):
+        sent.wait_recv()
+        passed.start()
+    for copy in to_mate + relay:
+        copy.wait_recv()
+
+    half_lane = lax.broadcasted_iota(jnp.int32, (quarter, 128), 1) < 64
+    for group in range(GROUPS):
+        low, high = group * PER_GROUP, (group + 1) * PER_GROUP
+        for_each(max(low, 1), high, lambda turn: outward(turn).wait_recv())
+        rows = arrived[pl.ds(group * quarter, quarter), :]
+        hidden = jnp.dot(rows, gate_up[...], preferred_element_type=jnp.float32)
+        active = []
+        for first in (0, 768):
+            blocks = [hidden[:, first + 128 * k : first + 128 * (k + 1)] for k in range(6)]
+            active.append(jnp.maximum(blocks[0], 0.0) * blocks[1])
+            active.append(jnp.maximum(blocks[3], 0.0) * blocks[4])
+            one, two = blocks[2], blocks[5]
+            gates = jnp.where(half_lane, one, pltpu.roll(two, 64, 1))
+            ups = jnp.where(half_lane, pltpu.roll(one, 64, 1), two)
+            active.append(jnp.maximum(gates, 0.0) * ups)
+        activated = jnp.concatenate(active, axis=1).astype(jnp.bfloat16)
+        results[pl.ds(group * quarter, quarter), :] = jnp.dot(
+            activated, down[...], preferred_element_type=jnp.float32
+        ).astype(jnp.bfloat16)
+        for_each(max(low, 1), high, lambda turn: homeward(turn).start())
+        if group == 0:
+            keep = pltpu.make_async_copy(
+                results.at[pl.ds(0, HALF_CAP)],
+                returned.at[pl.ds(mine, HALF_CAP)],
+                local_sem.at[1],
+            )
+            keep.start()
+
+    keep.wait()
+    for_each(1, ROUNDS, lambda turn: outward(turn).wait_send())
+    for copy in to_pair + to_mate + relay:
+        copy.wait_send()
+    for_each(1, ROUNDS, lambda turn: homeward(turn).wait())
+
+    gathered = jnp.dot(shares[...], returned[...], preferred_element_type=jnp.float32)
+    out_ref[...] = (
+        mid_ref[...].astype(jnp.float32) + gathered[:tokens] + gathered[tokens:]
+    ).astype(jnp.bfloat16)
+
+
+def run_experts(normed_moe, residual_mid, expert_ids, w_router, gate_up, down):
+    tokens, width = normed_moe.shape
+    vmem = pl.BlockSpec(memory_space=pltpu.VMEM)
+    return pl.pallas_call(
+        experts_kernel,
+        out_shape=jax.ShapeDtypeStruct((tokens, width), jnp.bfloat16),
+        in_specs=[vmem, vmem, vmem, vmem, pl.BlockSpec(memory_space=pl.ANY), pl.BlockSpec(memory_space=pl.ANY)],
+        out_specs=vmem,
+        scratch_shapes=[
+            pltpu.VMEM((SLOTS, width), jnp.bfloat16),
+            pltpu.VMEM((SLOTS, width), jnp.bfloat16),
+            pltpu.VMEM((SLOTS, width), jnp.bfloat16),
+            pltpu.VMEM((SLOTS, width), jnp.bfloat16),
+            pltpu.VMEM((width, 8 * SHARD), jnp.bfloat16),
+            pltpu.VMEM((4 * SHARD, width), jnp.bfloat16),
+            pltpu.VMEM((2 * tokens, SLOTS), jnp.bfloat16),
+            pltpu.SemaphoreType.DMA((ROUNDS,)),
+            pltpu.SemaphoreType.DMA((ROUNDS,)),
+            pltpu.SemaphoreType.DMA((ROUNDS,)),
+            pltpu.SemaphoreType.DMA((ROUNDS,)),
+            pltpu.SemaphoreType.DMA((3,)),
+            pltpu.SemaphoreType.DMA((9,)),
+            pltpu.SemaphoreType.DMA((9,)),
+        ],
+        compiler_params=pltpu.CompilerParams(
+            collective_id=1, has_side_effects=True, vmem_limit_bytes=60 << 20
+        ),
+    )(normed_moe, residual_mid, expert_ids, w_router, gate_up, down)
 
 
 def per_device(
@@ -187,39 +463,10 @@
     picked_kv = jax.vmap(take_rows)(fresh_kv, jnp.maximum(path, 0))
     compact_kv = jnp.where((path >= 0)[..., None], picked_kv, jnp.zeros((), jnp.bfloat16))
     normed_moe = rms_scale(residual_mid, moe_gain)
-    logits = jnp.dot(normed_moe, w_router, preferred_element_type=jnp.float32)
-    experts = w_router.shape[1]
-    split = device_count // experts
-    chosen = jnp.take_along_axis(logits, expert_ids, axis=1)
-    squashed = jax.nn.sigmoid(chosen)
-    gate_share = squashed / jnp.sum(squashed, axis=1, keepdims=True)
-    marks = expert_ids[:, :, None] == jnp.arange(experts, dtype=jnp.int32)[None, None, :]
-    assigned = jnp.sum(marks.astype(jnp.int32), axis=1)
-    ranks = jnp.cumsum(assigned, axis=0) - assigned
-    slot_ids = jnp.arange(CAP, dtype=jnp.int32)
-    dispatch_table = (
-        (ranks.T[:, None, :] == slot_ids[None, :, None]) & (assigned.T[:, None, :] > 0)
-    ).astype(jnp.bfloat16)
-    packed = jnp.einsum(
-        "ect,td->ecd", dispatch_table, normed_moe, preferred_element_type=jnp.float32
-    ).astype(jnp.bfloat16)
-    outgoing_rows = jnp.repeat(packed, split, axis=0)
-    tok_rows = lax.all_to_all(outgoing_rows, ("req", "ep"), split_axis=0, concat_axis=0, tiled=True)
-    flat_rows = tok_rows.reshape(-1, model_dim)
-    gate_val = jnp.dot(flat_rows, w_gate[0], preferred_element_type=jnp.float32)
-    up_val = jnp.dot(flat_rows, w_up[0], preferred_element_type=jnp.float32)
-    activated = (jnp.maximum(gate_val, 0.0) * up_val).astype(jnp.bfloat16)
-    result = jnp.dot(activated, w_down[0], preferred_element_type=jnp.float32).astype(jnp.bfloat16)
-    returned = lax.all_to_all(
-        result.reshape(tok_rows.shape), ("req", "ep"), split_axis=0, concat_axis=0, tiled=True
-    )
-    expert_out = jnp.sum(
-        returned.astype(jnp.float32).reshape(experts, split, CAP, model_dim), axis=1
-    ).reshape(experts * CAP, model_dim)
-    slot_pick = expert_ids * CAP + jnp.take_along_axis(ranks, expert_ids, axis=1)
-    gathered_rows = expert_out[slot_pick]
-    moe_sum = jnp.sum(gate_share[..., None] * gathered_rows, axis=1)
-    layer_out = (residual_mid.astype(jnp.float32) + moe_sum).astype(jnp.bfloat16)
+    gate_up = jnp.concatenate(
+        [w_gate[0, :, :128], w_up[0, :, :128], w_gate[0, :, 128:], w_up[0, :, 128:]], axis=1
+    )
+    layer_out = run_experts(normed_moe, residual_mid, expert_ids, w_router, gate_up, w_down[0])
     return (layer_out, compact_kv)
 
 

time: 534 us -> 241 us (0.45)
  waiting for transfers between devices: 228 us -> 36.6 us
  blocking collectives: 155 us -> 0 us
  Pallas kernels: 0 us -> 97.5 us
  matrix products: 37.9 us -> 18 us
  starting transfers between devices: 19.8 us -> 10.3 us
  local copies, waits for them, and re-layouts: 48.2 us -> 40.3 us
    all_to_all x1 -> x0, blocking collectives: 155 us -> none  [per_device(): lax.all_to_all(outgoing_rows, ('req', 'ep'), split_axis=0, concat_axis=0,...]
    all_to_all x1 -> x0, waiting for transfers between devices: 152 us -> none  [per_device(): lax.all_to_all(result.reshape(tok_rows.shape), ('req', 'ep'), split_axis=...]
    pallas_call x0 -> x1, Pallas kernels: none -> 97.5 us  [run_experts(): pl.pallas_call(experts_kernel, out_shape=jax.ShapeDtypeStruct((tokens, wi...]
    all_to_all x1, waiting for transfers between devices: 76.7 us -> 36.6 us  [per_device(): lax.all_to_all(outgoing, 'ep', split_axis=0, concat_axis=0, tiled=True)]
    dot_general x4 -> x0, matrix products: 22.6 us -> none  [the longest x1 13.6 us: per_device(): jnp.dot(activated, w_down[0], preferred_element_type=jnp.float32)]
    gather x10 -> x0, local copies, waits for them, and re-layouts: 20.4 us -> none  [the longest x2 12.4 us: per_device(): gathered_rows = expert_out[slot_pick]]
    reduce_sum x4 -> x0, other arithmetic: 14.4 us -> none  [the longest x1 10.2 us: per_device(): jnp.sum(returned.astype(jnp.float32).reshape(experts, split, CAP, model_d...]
    all_to_all x1 -> x0, starting transfers between devices: 9.51 us -> none  [per_device(): lax.all_to_all(result.reshape(tok_rows.shape), ('req', 'ep'), split_axis=...]
  transfers between devices with their start and end apart: 3 -> 2, of which waited for: 2 -> 1; matrix products, arithmetic and copies ran while one was open for 6% -> 26% of each run, Pallas kernels for 0% -> 0%
where the time goes in v1:
time: 241 us; the launch traced here: 238 us
  Pallas kernels  97.5 us (40%)
  local copies, waits for them, and re-layouts  40.3 us (17%)
  waiting for transfers between devices  36.6 us (15%)
  other arithmetic  31.2 us (13%)
  matrix products  18 us (7%)
  starting transfers between devices  10.3 us (4%)
  between operations  4.11 us (2%)
    pallas_call x1, Pallas kernels, run_experts(): pl.pallas_call(experts_kernel, out_shape=jax.ShapeDtypeStruct((tokens, wi...  97.5 us
    all_to_all x1, waiting for transfers between devices, per_device(): lax.all_to_all(outgoing, 'ep', split_axis=0, concat_axis=0, tiled=True)  36.6 us
    unnamed x50, local copies, waits for them, and re-layouts  14.3 us
    all_to_all x1, starting transfers between devices, per_device(): lax.all_to_all(length_out, 'ep', split_axis=0, concat_axis=0, tiled=True)  5.23 us
    dot_general x2, matrix products, attend(): jnp.einsum('kgsl,lkd->kgsd', weights, value_head_rows.astype(jnp.float32)...  5.1 us
    all_to_all x1, starting transfers between devices, per_device(): lax.all_to_all(outgoing, 'ep', split_axis=0, concat_axis=0, tiled=True)  5.03 us
  transfers between devices with their start and end apart: 2, of which 1 were waited for; matrix products, arithmetic and copies ran while one was open for 26% of the time, Pallas kernels for 0%

profile of v1, /device:TPU:9, one launch (start us, length us, event | category | flops | bytes accessed | tf_op | source)
XLA Modules:
  0.0 238.0 jit_solution(5022743496314991896)
XLA Ops:
  0.6 0.8 copy.142
  3.4 1.2 compare_select_fusion
  4.6 5.2 %all-to-all-start = ((s32[8,1,1]{2,1,0:T(1,128)}), s32[8,1,1]{2,1,0:T(1,128)S(1)}, u32[]{:S(2)}, u32[]{:S(2)}) async-start(s32[8,1,1]{2,1,0:T(1,128)} %compare_select_fusion), calls=%async_computation | async-start | bytes 8192 | tf_op jit(solution)/shard_map/all_to_all | solution.py:409
  10.6 2.0 gather_fusion
  12.6 1.3 dynamic-slice_bitcast_fusion
  13.9 3.8 %broadcast_select_fusion = bf16[8,1024,512]{2,1,0:T(8,128)(2,1)} fusion(pred[8]{0:T(512)(128)(4,1)S(1)} %iota_compare_fusion.4, bf16[1024,512]{1,0:T(8,128)(2,1)S(1)} %dynamic-slice_bitcast_fusion), kind=kLoop, calls=%fused_computation.2 | loop fusion | flops 4194304 | bytes 9437192 | tf_op jit(solution)/shard_map/jit(_where)/select_n | solution.py:405
  17.8 5.0 %all-to-all-start.1 = ((bf16[8,1024,512]{2,1,0:T(8,128)(2,1)}), bf16[8,1024,512]{2,1,0:T(8,128)(2,1)}, u32[]{:S(2)}, u32[]{:S(2)}) async-start(bf16[8,1024,512]{2,1,0:T(8,128)(2,1)} %broadcast_select_fusion), calls=%async_computation.1 | async-start | bytes 16777216 | tf_op jit(solution)/shard_map/all_to_all | solution.py:408
  23.0 4.0 %fusion.28 = f32[128,2048]{1,0:T(8,128)S(1)} fusion(bf16[1536,2048]{1,0:T(8,128)(2,1)} %param.30, bf16[128,1536]{1,0:T(8,128)(2,1)S(1)} %copy-done.1, f32[1536]{0:T(1024)S(1)} %convert_element_type.54, f32[128]{0:T(128)S(1)} %add_rsqrt_fusion.1), kind=kOutput, calls=%fused_computation.48 | convolution fusion | flops 806092800 | bytes 7739904 | tf_op jit(solution)/shard_map/dot_general | solution.py:402
  27.0 1.0 slice.86
  30.0 0.8 slice.78
  31.5 0.8 slice.77
  32.3 1.3 reshape.217
  34.7 0.9 fusion.56
  36.1 1.4 copy.96
  37.5 1.6 reshape.219
  39.2 1.5 reshape.220
  40.7 1.4 copy.106.ids_ref
  42.1 1.8 copy.107.router_ref
  43.9 1.8 copy.127
  45.7 1.9 copy.126
  47.6 1.9 copy.125
  49.5 1.9 copy.124
  51.5 1.2 bitcast_or_fusion
  54.1 1.4 and_reduce_fusion
  55.4 1.3 broadcast_compare_fusion.1
  56.7 1.8 fusion.55
  58.5 2.7 %pad_maximum_fusion.gate_up_ref = bf16[1536,384]{1,0:T(8,128)(2,1)} fusion(bf16[1536,64]{1,0:T(8,128)(2,1)} %bitcast.122, bf16[1536,64]{1,0:T(8,128)(2,1)} %bitcast.123, bf16[1536,128]{1,0:T(8,128)(2,1)} %bitcast.124, bf16[1536,128]{1,0:T(8,128)(2,1)} %bitcast.125), kind=kLoop, calls=%fused_computation.27 | loop fusion | flops 4718592 | bytes 2359296 | tf_op jit(solution)/shard_map/concatenate | solution.py:466
  63.9 2.5 %fusion.46 = s32[2]{0:T(128)} fusion(s32[2]{0:T(128)} %copy-done.19, s32[]{:T(128)} %select_n.52, s32[1]{0:T(128)} %bitcast.4, s32[1]{0:T(128)} %dynamic_slice.12, s32[1]{0:T(128)} %bitcast.1), kind=kLoop, calls=%fused_computation.97 | loop fusion | flops 4 | bytes 2056 | tf_op jit(solution)/shard_map/scatter | solution.py:412
  67.8 1.0 multiply_cosine_fusion
  70.2 1.0 multiply_subtract_fusion
  71.4 0.9 pad_maximum_fusion.2
  72.2 2.0 gather_fusion.1
  74.2 1.3 fusion.57
  75.5 0.9 copy-done.5
  77.2 1.6 broadcast_select_fusion.1
  78.9 36.6 %all-to-all-done.1 = bf16[8,1024,512]{2,1,0:T(8,128)(2,1)} async-done(((bf16[8,1024,512]{2,1,0:T(8,128)(2,1)}), bf16[8,1024,512]{2,1,0:T(8,128)(2,1)}, u32[]{:S(2)}, u32[]{:S(2)}) %all-to-all-start.1) | async-done | bytes 8388640 | tf_op jit(solution)/shard_map/all_to_all | solution.py:408
  115.5 3.4 %select_dynamic-update-slice_fusion = bf16[2,1024,512]{2,1,0:T(8,128)(2,1)} fusion(bf16[2,1024,512]{2,1,0:T(8,128)(2,1)} %bitcast.113, s32[]{:T(128)} %select_n.52, bf16[8,1024,512]{2,1,0:T(8,128)(2,1)} %all-to-all-done.1, s32[]{:T(128)S(6)} %select_n.58, pred[]{:T(512)} %and_reduce_fusion), kind=kLoop, calls=%fused_computation.36 | loop fusion | flops 524288 | bytes 3146756 | tf_op jit(solution)/shard_map/scatter | solution.py:413
  118.9 2.7 %fusion.54 = (bf16[2,1024,256]{2,1,0:T(8,128)(2,1)}, bf16[2,1024,256]{2,1,0:T(8,128)(2,1)S(1)}) fusion(bf16[2,1024,512]{2,1,0:T(8,128)(2,1)} %select_dynamic-update-slice_fusion), kind=kLoop, calls=%fused_computation.103 | loop fusion | bytes 4194304 | tf_op jit(solution)/shard_map/slice | solution.py:60
  121.6 1.3 copy.94
  122.9 1.5 copy.88
  124.4 2.5 %bitcast_reduce_fusion = (f32[2,2,6,64]{3,2,1,0:T(8,128)S(1)}, f32[2,2,1024,64,6]{2,3,4,1,0:T(8,128)S(1)}) fusion(pred[2,1024]{1,0:T(4,128)(4,1)S(1)} %iota_compare_fusion.3, bf16[2,1024,2,128,1]{1,3,4,2,0:T(8,128)(2,1)S(1)} %bitcast.114, bf16[2,64,2,6,64]{4,1,3,2,0:T(8,128)(2,1)} %bitcast.119, bf16[2,64,2,6,64]{4,1,3,2,0:T(8,128)(2,1)} %bitcast.121), kind=kOutput, calls=%fused_computation.4 | convolution fusion | flops 408156672 | bytes 7741440 | tf_op jit(solution)/shard_map/vmap(skgd,lkd->kgsl)/dot_general | solution.py:66
  126.9 1.8 fusion.1
  128.7 4.0 %fusion.17 = f32[2,64,2,6,128]{4,1,3,2,0:T(8,128)S(1)} fusion(bf16[2,1024,2,128,1]{1,3,4,2,0:T(8,128)(2,1)S(1)} %bitcast.126, f32[2,2,1024,64,6]{2,3,4,1,0:T(8,128)S(1)} %get-tuple-element.42, f32[2,2,6,64]{3,2,1,0:T(8,128)S(1)} %get-tuple-element.41, pred[2,1024]{1,0:T(4,128)(4,1)S(1)} %iota_compare_fusion.3, f32[2,64,2,6]{1,3,2,0:T(8,128)S(1)} %get-tuple-element.28), kind=kOutput, calls=%fused_computation.23 | convolution fusion | flops 2420834304 | bytes 8140800 | tf_op jit(solution)/shard_map/vmap(kgsl,lkd->kgsd)/dot_general | solution.py:73
  132.7 1.1 fusion.20
  134.6 3.2 %fusion.21 = (f32[128]{0:T(128)S(1)}, bf16[128,1536]{1,0:T(8,128)(2,1)S(1)}) fusion(bf16[128,1536]{1,0:T(8,128)(2,1)S(1)} %convert_element_type.61, bf16[1536,1536]{1,0:T(8,128)(2,1)} %param.31, bf16[128,1536]{1,0:T(8,128)(2,1)S(1)} %copy-done.1), kind=kOutput, calls=%fused_computation.40 | convolution fusion | flops 605159296 | bytes 5898752 | tf_op jit(solution)/shard_map/dot_general | solution.py:454
  137.8 0.9 fusion.23.normed_ref
  138.7 97.5 %shard_map.176 = bf16[128,1536]{1,0:T(8,128)(2,1)} custom-call(bf16[128,1536]{1,0:T(8,128)(2,1)} %fusion.23.normed_ref, bf16[128,1536]{1,0:T(8,128)(2,1)} %copy-done.4, s32[128,4]{1,0:T(8,128)} %copy.106.ids_ref, bf16[1536,32]{1,0:T(8,128)(2,1)} %copy.107.router_ref, bf16[1536,384]{1,0:T(8,128)(2,1)} %pad_maximum_fusion.gate_up_ref, bf16[192,1536]{1,0:T(8,128)(2,1)} %bitcast.127), custom_call_target="tpu_custom_call" | custom-call | tf_op jit(solution)/shard_map/pallas_call | solution.py:335
  236.2 1.8 copy.143
  (79 shorter events, 12.7 us)
Async XLA Ops:
  0.6 10.0 %copy-start = (bf16[16,128,512]{2,1,0:T(8,128)(2,1)S(1)}, bf16[16,128,512]{2,1,0:T(8,128)(2,1)}, u32[]{:S(2)}) copy-start(bf16[16,128,512]{2,1,0:T(8,128)(2,1)} %param.26) | copy-start | bytes 6291460
  1.5 3.1 %copy-start.19 = (s32[2]{0:T(128)}, s32[2]{0:T(128)S(1)}, u32[]{:S(2)}) copy-start(s32[2]{0:T(128)S(1)} %copy.142) | copy-start | bytes 28
  4.6 13.2 %all-to-all-start = ((s32[8,1,1]{2,1,0:T(1,128)}), s32[8,1,1]{2,1,0:T(1,128)S(1)}, u32[]{:S(2)}, u32[]{:S(2)}) async-start(s32[8,1,1]{2,1,0:T(1,128)} %compare_select_fusion), calls=%async_computation | async-start | bytes 8192 | tf_op jit(solution)/shard_map/all_to_all | solution.py:409
  17.8 5.0 %copy-start.16 = (bf16[1536]{0:T(1024)(128)(2,1)S(1)}, bf16[1536]{0:T(1024)(128)(2,1)}, u32[]{:S(2)}) copy-start(bf16[1536]{0:T(1024)(128)(2,1)} %param.29) | copy-start | bytes 9220
  17.8 5.1 %copy-start.1 = (bf16[128,1536]{1,0:T(8,128)(2,1)S(1)}, bf16[128,1536]{1,0:T(8,128)(2,1)}, u32[]{:S(2)}) copy-start(bf16[128,1536]{1,0:T(8,128)(2,1)} %param.21) | copy-start | bytes 1179652
  17.8 97.7 %all-to-all-start.1 = ((bf16[8,1024,512]{2,1,0:T(8,128)(2,1)}), bf16[8,1024,512]{2,1,0:T(8,128)(2,1)}, u32[]{:S(2)}, u32[]{:S(2)}) async-start(bf16[8,1024,512]{2,1,0:T(8,128)(2,1)} %broadcast_select_fusion), calls=%async_computation.1 | async-start | bytes 16777216 | tf_op jit(solution)/shard_map/all_to_all | solution.py:408
  22.8 6.5 %copy-start.8 = (bf16[1,1536,192]{1,2,0:T(8,128)(2,1)S(1)}, bf16[1,1536,192]{1,2,0:T(8,128)(2,1)}, u32[]{:S(2)}) copy-start(bf16[1,1536,192]{1,2,0:T(8,128)(2,1)} %param.36) | copy-start | bytes 1769476
  22.8 8.0 %copy-start.9 = (bf16[1,1536,192]{1,2,0:T(8,128)(2,1)S(1)}, bf16[1,1536,192]{1,2,0:T(8,128)(2,1)}, u32[]{:S(2)}) copy-start(bf16[1,1536,192]{1,2,0:T(8,128)(2,1)} %param.35) | copy-start | bytes 1769476
  23.0 10.5 %copy-start.18 = (s32[2,64]{1,0:T(2,128)S(1)}, s32[2,64]{1,0:T(2,128)}, u32[]{:S(2)}) copy-start(s32[2,64]{1,0:T(2,128)} %param.22) | copy-start | bytes 1540
  23.0 17.6 %copy-start.17 = (bf16[1536]{0:T(1024)(128)(2,1)S(1)}, bf16[1536]{0:T(1024)(128)(2,1)}, u32[]{:S(2)}) copy-start(bf16[1536]{0:T(1024)(128)(2,1)} %param.32) | copy-start | bytes 9220
  68.8 0.7 copy-start.10
  68.8 0.7 copy-start.11
  68.8 8.4 %copy-start.20 = (s32[2]{0:T(128)S(1)}, s32[2]{0:T(128)}, u32[]{:S(2)}) copy-start(s32[2]{0:T(128)} %fusion.46) | copy-start | bytes 28
  69.5 46.0 %copy-start.2 = (bf16[2,64,12,64]{3,1,2,0:T(8,128)(2,1)}, bf16[2,64,12,64]{3,1,2,0:T(8,128)(2,1)S(1)}, u32[]{:S(2)}) copy-start(bf16[2,64,12,64]{3,1,2,0:T(8,128)(2,1)S(1)} %copy.92) | copy-start | bytes 589828
  69.6 45.9 %copy-start.3 = (bf16[2,64,12,64]{3,1,2,0:T(8,128)(2,1)}, bf16[2,64,12,64]{3,1,2,0:T(8,128)(2,1)S(1)}, u32[]{:S(2)}) copy-start(bf16[2,64,12,64]{3,1,2,0:T(8,128)(2,1)S(1)} %copy.91) | copy-start | bytes 589828
  75.5 0.9 copy-start.5
  75.5 1.6 copy-start.12
  124.4 4.3 %copy-start.13 = (f32[2,2,6,64]{3,2,1,0:T(8,128)S(1)}, f32[2,2,6,64]{3,2,1,0:T(8,128)}, u32[]{:S(2)}) copy-start(f32[2,2,6,64]{3,2,1,0:T(8,128)} %copy-done.12) | copy-start | bytes 18436
  124.4 4.3 %copy-start.14 = (f32[2,2,6,64]{3,2,1,0:T(8,128)S(1)}, f32[2,2,6,64]{3,2,1,0:T(8,128)}, u32[]{:S(2)}) copy-start(f32[2,2,6,64]{3,2,1,0:T(8,128)} %fusion.27) | copy-start | bytes 18436
  124.4 4.3 %copy-start.7 = (bf16[2,1024,256]{1,2,0:T(8,128)(2,1)S(1)}, bf16[2,1024,256]{1,2,0:T(8,128)(2,1)}, u32[]{:S(2)}) copy-start(bf16[2,1024,256]{1,2,0:T(8,128)(2,1)} %copy.94) | copy-start | bytes 3145732
  128.7 4.0 %copy-start.6 = (f32[2,2,6,64,64]{3,4,2,1,0:T(8,128)S(1)}, f32[2,2,6,64,64]{3,4,2,1,0:T(8,128)}, u32[]{:S(2)}) copy-start(f32[2,2,6,64,64]{3,4,2,1,0:T(8,128)} %copy-done.5) | copy-start | bytes 1179652
  128.7 4.0 %copy-start.15 = (bf16[2,64,2,128]{3,2,1,0:T(2,128)(2,1)S(1)}, bf16[2,64,2,128]{3,2,1,0:T(2,128)(2,1)}, u32[]{:S(2)}) copy-start(bf16[2,64,2,128]{3,2,1,0:T(2,128)(2,1)} %reshape.220) | copy-start | bytes 196612
  137.8 0.9 copy-start.4
